TPU v7x, 512 devices: a whole 4x4x16 slice. The times are simulated.
512 devices in a mesh: dp: 32 (over z, core), expert: 16 (over x, y).
Axes of the slice: x: 4, y: 4, z: 16, core: 2. Of those that a mesh axis runs over, the one named last changes fastest.
Arguments:
- cached_hidden: bfloat16 [65536, 1536], P(('dp', 'expert')), may hold values from -6 to 6
- direction: bfloat16 [16, 2880, 1536], P('expert', 'dp'), may hold values from -1 to 1
- expert_ids: int32 [65536, 4], P(('dp', 'expert')), may hold values from 0 to 127, as said below
- gate_weights: float32 [65536, 4], P(('dp', 'expert')), may hold values from 0.05 to 1
Outputs:
- curvature_product: float32 [16, 2880, 1536], P('expert', 'dp')
Inputs may be any that keep to these rules, and one draw needn't show every extreme that they name: `expert_ids`: each row names 4 different experts, at most two of them below 16. Among the 128 rows of one device no expert below 16 is named more than 8 times; for every dp index, some expert below 16 is named exactly 8 times by the rows of each device with that dp index.
All inputs are finite; a program needn't handle non-finite values.
Results may differ from a plain program's by a relative error of at most 0.0034.
Values may be sent and summed in bfloat16 or wider, within the bound.
No kernel may reach another device: no remote copies, remote signals or barrier semaphores. Data moves between devices by JAX's collectives and lax.ppermute only.
A program may use at most 128 MiB of HBM per device.

v0:
```python
import math

import jax
import jax.numpy as jnp
from jax import lax
from jax.sharding import PartitionSpec as P


def slot_positions(block_ids, experts):
    flat = block_ids.reshape(-1)
    onehot = (flat[:, None] == jnp.arange(experts, dtype=jnp.int32)[None, :]).astype(jnp.int32)
    before = jnp.cumsum(onehot, axis=0) - onehot
    return jnp.sum(before * onehot, axis=1).reshape(block_ids.shape)


def body(cached_hidden, direction, expert_ids, gate_weights):
    dp_count = lax.axis_size("dp")
    owner_count = lax.axis_size("expert")
    slot_rows = cached_hidden.shape[0]
    capacity = slot_rows // owner_count
    tok_count = expert_ids.shape[0]
    width = direction.shape[1] * dp_count
    local_dir = direction[0]
    rows_all = lax.all_gather(cached_hidden, "dp", axis=0, tiled=True)
    tangent = lax.dot_general(
        rows_all, local_dir, (((1,), (1,)), ((), ())), preferred_element_type=jnp.float32
    )
    tangent = tangent.astype(jnp.bfloat16).reshape(
        dp_count, owner_count, capacity, local_dir.shape[0]
    )
    returned = lax.all_to_all(
        lax.all_to_all(tangent, "dp", split_axis=0, concat_axis=3, tiled=True),
        "expert",
        split_axis=1,
        concat_axis=1,
        tiled=True,
    )
    flat_rows = returned.reshape(owner_count * capacity, width)
    treated = expert_ids < owner_count
    slot_pos = slot_positions(expert_ids, owner_count)
    target = expert_ids * capacity + slot_pos
    lookup = jnp.where(treated, target, 0).reshape(-1)
    dropped = jnp.where(treated, target, owner_count * capacity).reshape(-1)
    gates = jnp.where(treated, gate_weights, 0.0)
    picked = jnp.take(flat_rows, lookup, axis=0).reshape(tok_count, expert_ids.shape[1], width)
    scale_factor = 1.0 / math.sqrt(tok_count * dp_count * owner_count)
    combined = jnp.sum(gates[..., None] * picked.astype(jnp.float32), axis=1) * scale_factor
    outgoing = (gates[..., None] * combined[:, None, :]).astype(jnp.bfloat16)
    buffer = jnp.zeros((owner_count * capacity, width), jnp.bfloat16)
    buffer = buffer.at[dropped].set(outgoing.reshape(-1, width), mode="drop")
    buffer = buffer.reshape(1, owner_count, capacity, width)
    arrived = lax.all_to_all(buffer, "expert", split_axis=1, concat_axis=1, tiled=True)
    adjoint = lax.all_to_all(arrived, "dp", split_axis=3, concat_axis=0, tiled=True)
    adjoint_rows = adjoint.reshape(-1, adjoint.shape[3])
    gradient = lax.dot_general(
        adjoint_rows, rows_all, (((0,), (0,)), ((), ())), preferred_element_type=jnp.float32
    )
    return gradient.reshape(1, gradient.shape[0], gradient.shape[1])


def solution(mesh):
    return jax.shard_map(
        body,
        mesh=mesh,
        in_specs=(
            P(("dp", "expert"), None),
            P("expert", "dp", None),
            P(("dp", "expert"), None),
            P(("dp", "expert"), None),
        ),
        out_specs=P("expert", "dp", None),
        check_vma=False,
    )
```

profile of v0, /device:TPU:1, one launch (start us, length us, event | category | flops | bytes accessed | tf_op | source)
XLA Modules:
  0.0 336.8 jit_solution(6748889101096679168)
XLA Ops:
  6.5 0.0 copy-start
  6.5 0.0 all-gather.2.cloned.1.call-start
  6.5 0.7 all-gather.2.cloned.1.call-update
  7.3 95.0 %all-gather.2.cloned.1.call-done = bf16[4096,1536]{1,0:T(8,128)(2,1)} async-done(((bf16[128,1536]{1,0:T(8,128)(2,1)}), bf16[4096,1536]{1,0:T(8,128)(2,1)}) %all-gather.2.cloned.1.call-update) | async-done | bytes 12582928 | tf_op jit(solution)/shard_map/all_gather | solution.py:24
  102.3 0.0 copy-done
  102.3 8.5 %convolution_convert_fusion = bf16[4096,90]{0,1:T(8,128)(2,1)S(1)} fusion(bf16[4096,1536]{1,0:T(8,128)(2,1)} %all-gather.2.cloned.1.call-done, bf16[1,90,1536]{2,1,0:T(8,128)(2,1)S(1)} %copy-done), kind=kOutput, calls=%fused_computation.4 | convolution fusion | flops 1132830720 | bytes 13596672 | tf_op jit(solution)/shard_map/dot_general | solution.py:25
  110.7 0.0 copy-start.1
  110.7 0.0 copy-start.2
  110.8 1.4 copy.65
  112.2 7.8 %all-to-all-start = ((bf16[32,16,8,90]{3,2,1,0:T(8,128)(2,1)}), bf16[32,16,8,90]{3,2,1,0:T(8,128)(2,1)S(1)}, u32[]{:S(2)}, u32[]{:S(2)}) async-start(bf16[32,16,8,90]{3,2,1,0:T(8,128)(2,1)} %bitcast.3), calls=%async_computation | async-start | bytes 2097152 | tf_op jit(solution)/shard_map/all_to_all | solution.py:32
  120.0 0.0 copy-done.1
  120.0 0.1 copy.57
  120.1 0.1 eq.29
  120.2 0.1 eq.25
  120.3 0.0 copy-done.2
  120.4 0.1 copy.62
  120.5 0.1 mul.48
  120.6 1.2 reduce-window.6
  121.7 0.2 slice_reduce_fusion
  122.0 0.1 fusion.6
  122.1 0.1 reshape.119
  122.2 0.1 copy.60
  122.3 0.1 copy.64
  122.5 53.2 %all-to-all-done = bf16[32,16,8,90]{3,2,1,0:T(8,128)(2,1)S(1)} async-done(((bf16[32,16,8,90]{3,2,1,0:T(8,128)(2,1)}), bf16[32,16,8,90]{3,2,1,0:T(8,128)(2,1)S(1)}, u32[]{:S(2)}, u32[]{:S(2)}) %all-to-all-start) | async-done | bytes 737312 | tf_op jit(solution)/shard_map/all_to_all | solution.py:32
  175.7 0.7 copy.66
  176.4 2.9 all_to_all.33
  179.3 6.5 %all-to-all-start.1 = ((bf16[1,16,8,2880]{3,2,0,1:T(8,128)(2,1)}), bf16[1,16,8,2880]{3,2,0,1:T(8,128)(2,1)S(1)}, u32[]{:S(2)}, u32[]{:S(2)}) async-start(bf16[1,16,8,2880]{3,2,0,1:T(8,128)(2,1)} %bitcast.6), calls=%async_computation.1 | async-start | bytes 1507328 | tf_op jit(solution)/shard_map/all_to_all | solution.py:31
  185.8 0.1 copy.61
  185.9 0.1 reshape.120
  186.0 0.1 copy.68
  186.1 0.1 reshape.123
  186.3 11.9 %all-to-all-done.1 = bf16[1,16,8,2880]{3,2,0,1:T(8,128)(2,1)S(1)} async-done(((bf16[1,16,8,2880]{3,2,0,1:T(8,128)(2,1)}), bf16[1,16,8,2880]{3,2,0,1:T(8,128)(2,1)S(1)}, u32[]{:S(2)}, u32[]{:S(2)}) %all-to-all-start.1) | async-done | bytes 737312 | tf_op jit(solution)/shard_map/all_to_all | solution.py:31
  198.2 3.7 %gather_fusion = bf16[512,2880]{1,0:T(8,128)(2,1)} fusion(bf16[128,2880]{1,0:T(8,128)(2,1)S(1)} %bitcast.44, s32[1024]{0:T(1024)S(1)} %pad_clamp_fusion), kind=kCustom, calls=%fused_computation | custom fusion | bytes 5900288 | tf_op jit(solution)/shard_map/jit(_take)/gather | solution.py:45
  201.9 4.7 %gather.7 = bf16[128,4,2880]{2,1,0:T(4,128)(2,1)S(1)} reshape(bf16[512,2880]{1,0:T(8,128)(2,1)} %gather_fusion) | data formatting | bytes 5898240 | tf_op jit(solution)/shard_map/jit(_take)/gather | solution.py:45
  206.6 6.3 %multiply_reduce_fusion = f32[128,2880]{1,0:T(8,128)S(1)} fusion(bf16[128,4,2880]{2,1,0:T(4,128)(2,1)S(1)} %gather.7, f32[128,4]{1,0:T(8,128)S(1)} %copy.62, pred[128,4]{1,0:T(8,128)(4,1)S(1)} %copy.64), kind=kLoop, calls=%fused_computation.3 | loop fusion | flops 5529600 | bytes 4426240 | tf_op jit(solution)/shard_map/reduce_sum | solution.py:47
  212.9 0.1 broadcast_multiply_fusion
  213.0 3.6 %mul.54 = f32[128,4,2880]{2,1,0:T(4,128)} broadcast(f32[128,2880]{1,0:T(8,128)S(1)} %broadcast_multiply_fusion), dimensions={0,2} | broadcast | bytes 7372800 | tf_op jit(solution)/shard_map/mul | solution.py:48
  216.5 7.7 %mul.55 = f32[512,2880]{1,0:T(8,128)} reshape(f32[128,4,2880]{2,1,0:T(4,128)} %mul.54) | data formatting | bytes 11796480 | tf_op jit(solution)/shard_map/mul | solution.py:48
  224.3 7.1 %scatter_custom_fusion = bf16[128,2880]{1,0:T(8,128)(2,1)S(1)} fusion(s32[512]{0:T(512)S(1)} %bitcast.52, f32[512,2880]{1,0:T(8,128)} %mul.55, f32[512]{0:T(512)S(1)} %mul.48, bf16[]{:T(256)} %constant.9.clone.1), kind=kCustom, calls=%fused_computation.5 | custom fusion | flops 2949120 | bytes 6637570 | tf_op jit(solution)/shard_map/scatter | solution.py:50
  231.4 15.4 %all_to_all.43 = bf16[1,16,8,2880]{3,2,0,1:T(8,128)(2,1)S(1)} all-to-all(bf16[1,16,8,2880]{3,2,0,1:T(8,128)(2,1)S(1)} %bitcast.50), channel_id=1, replica_groups=mesh['dp'=32,'expert'=16] {'expert'}, dimensions={1} | all-to-all | bytes 1474560 | tf_op jit(solution)/shard_map/all_to_all | solution.py:52
  246.8 5.5 %copy.69 = bf16[1,16,8,2880]{1,2,0,3:T(8,128)(2,1)} copy(bf16[1,16,8,2880]{3,2,0,1:T(8,128)(2,1)S(1)} %all_to_all.43) | data formatting | bytes 1474560 | tf_op jit(solution)/shard_map/all_to_all | solution.py:52
  252.4 8.5 %reshape.146 = bf16[32,2,5760]{2,1,0:T(2,128)(2,1)S(1)} reshape(bf16[2880,1,8,16]{3,2,1,0:T(8,128)(2,1)} %bitcast.45) | data formatting | bytes 1474560
  260.9 48.5 %all_to_all.44 = bf16[32,2,5760]{2,1,0:T(2,128)(2,1)S(1)} all-to-all(bf16[32,2,5760]{2,1,0:T(2,128)(2,1)S(1)} %reshape.146), channel_id=1, replica_groups=mesh['dp'=32,'expert'=16] {'dp'}, dimensions={0} | all-to-all | bytes 1474560 | tf_op jit(solution)/shard_map/all_to_all | solution.py:53
  309.4 5.5 %reshape.147 = bf16[2880,1,8,16]{3,2,1,0:T(8,128)(2,1)} reshape(bf16[32,2,5760]{2,1,0:T(2,128)(2,1)S(1)} %all_to_all.44) | data formatting | bytes 1474560
  314.9 6.5 %copy.73 = bf16[1,16,8,32,90]{4,3,2,1,0:T(8,128)(2,1)S(1)} copy(bf16[1,16,8,32,90]{1,2,4,3,0:T(8,128)(2,1)} %bitcast.46) | data formatting | bytes 1474560 | tf_op jit(solution)/shard_map/all_to_all | solution.py:53
  321.4 0.4 copy.71
  321.9 6.7 %convolution_bitcast_fusion = f32[1,90,1536]{2,1,0:T(8,128)S(1)} fusion(bf16[4096,90]{1,0:T(8,128)(2,1)S(1)} %bitcast.47, bf16[4096,1536]{1,0:T(8,128)(2,1)} %all-gather.2.cloned.1.call-done), kind=kOutput, calls=%fused_computation.7 | convolution fusion | flops 1132462080 | bytes 13873152 | tf_op jit(solution)/shard_map/dot_general | solution.py:55
  328.6 1.4 copy.72
  (9 shorter events, 0.1 us)
Async XLA Ops:
  6.5 95.7 %copy-start = (bf16[1,90,1536]{2,1,0:T(8,128)(2,1)S(1)}, bf16[1,90,1536]{2,1,0:T(8,128)(2,1)}, u32[]{:S(2)}) copy-start(bf16[1,90,1536]{2,1,0:T(8,128)(2,1)} %param.5) | copy-start | bytes 829444
  6.5 95.7 %all-gather.2.cloned.1.call-start = ((), (), s32[]{:S(2)}) async-start(), calls=%async_computation.4 | async-start | bytes 12976128 | tf_op jit(solution)/shard_map/all_gather | solution.py:24
  110.7 9.3 %copy-start.1 = (s32[128,4]{0,1:T(4,128)S(1)}, s32[128,4]{0,1:T(4,128)}, u32[]{:S(2)}) copy-start(s32[128,4]{0,1:T(4,128)} %param.6) | copy-start | bytes 6148
  110.7 9.6 %copy-start.2 = (f32[128,4]{0,1:T(4,128)S(1)}, f32[128,4]{0,1:T(4,128)}, u32[]{:S(2)}) copy-start(f32[128,4]{0,1:T(4,128)} %param.7) | copy-start | bytes 6148
  112.2 63.5 %all-to-all-start = ((bf16[32,16,8,90]{3,2,1,0:T(8,128)(2,1)}), bf16[32,16,8,90]{3,2,1,0:T(8,128)(2,1)S(1)}, u32[]{:S(2)}, u32[]{:S(2)}) async-start(bf16[32,16,8,90]{3,2,1,0:T(8,128)(2,1)} %bitcast.3), calls=%async_computation | async-start | bytes 2097152 | tf_op jit(solution)/shard_map/all_to_all | solution.py:32
  179.3 19.0 %all-to-all-start.1 = ((bf16[1,16,8,2880]{3,2,0,1:T(8,128)(2,1)}), bf16[1,16,8,2880]{3,2,0,1:T(8,128)(2,1)S(1)}, u32[]{:S(2)}, u32[]{:S(2)}) async-start(bf16[1,16,8,2880]{3,2,0,1:T(8,128)(2,1)} %bitcast.6), calls=%async_computation.1 | async-start | bytes 1507328 | tf_op jit(solution)/shard_map/all_to_all | solution.py:31
Sparse Core Ops, SparseCore 0:
  9.5 92.7 all-gather.1
where the time goes:
time: 338 us; the launch traced here: 337 us
  waiting for transfers between devices  161 us (48%)
  blocking collectives  63.9 us (19%)
  local copies, waits for them, and re-layouts  54 us (16%)
  matrix products  15.2 us (4%)
  other arithmetic  14.9 us (4%)
  starting transfers between devices  14.3 us (4%)
  between operations  13.6 us (4%)
    all_gather x1, waiting for transfers between devices, body(): rows_all = lax.all_gather(cached_hidden, 'dp', axis=0, tiled=True)  95 us
    all_to_all x1, waiting for transfers between devices, body(): lax.all_to_all(tangent, 'dp', split_axis=0, concat_axis=3, tiled=True)  53.2 us
    all_to_all x1, blocking collectives, body(): lax.all_to_all(arrived, 'dp', split_axis=3, concat_axis=0, tiled=True)  48.5 us
    all_to_all x1, blocking collectives, body(): lax.all_to_all(buffer, 'expert', split_axis=1, concat_axis=1, tiled=True)  15.4 us
    unnamed x9, local copies, waits for them, and re-layouts  14.2 us
    all_to_all x1, waiting for transfers between devices, body(): lax.all_to_all(lax.all_to_all(tangent, 'dp', split_axis=0, concat_axis=3,...  11.9 us
    mul x3, local copies, waits for them, and re-layouts, body(): outgoing = (gates[..., None] * combined[:, None, :]).astype(jnp.bfloat16)  11.4 us
    dot_general x1, matrix products, body(): lax.dot_general(rows_all, local_dir, (((1,), (1,)), ((), ())), preferred_...  8.46 us
  transfers between devices with their start and end apart: 3, of which 3 were waited for; matrix products, arithmetic and copies ran while one was open for 1% of the time, Pallas kernels for 0%

commit v1 on v0

v1 whole, which is shorter than its diff:
```python
import math

import jax
import jax.numpy as jnp
from jax import lax
from jax.sharding import PartitionSpec as P

CHUNKS = 4


def slot_tables(expert_ids, gate_weights, experts, capacity):
    topk = expert_ids.shape[1]
    ids = expert_ids.reshape(-1)
    pairs = ids.shape[0]
    index = jnp.arange(pairs, dtype=jnp.int32)
    onehot = (ids[:, None] == jnp.arange(experts, dtype=jnp.int32)[None, :]).astype(jnp.float32)
    earlier = (index[None, :] < index[:, None]).astype(jnp.bfloat16)
    before = jnp.dot(earlier, onehot.astype(jnp.bfloat16), preferred_element_type=jnp.float32)
    position = jnp.sum(before * onehot, axis=1).astype(jnp.int32)
    slot = jnp.where(ids < experts, ids * capacity + position, -1)
    holds = slot[:, None] == jnp.arange(experts * capacity, dtype=jnp.int32)[None, :]
    token = (index // topk).astype(jnp.float32)
    gates = gate_weights.reshape(-1)
    tokens = jnp.sum(jnp.where(holds, token[:, None], 0.0), axis=0)
    weights = jnp.sum(jnp.where(holds, gates[:, None], 0.0), axis=0)
    return jnp.stack([tokens, weights])


def body(cached_hidden, direction, expert_ids, gate_weights):
    rows = lax.axis_size("dp")
    experts = lax.axis_size("expert")
    capacity = cached_hidden.shape[0] // experts
    tok_count = expert_ids.shape[0]
    scale = 1.0 / math.sqrt(tok_count * rows * experts)
    local_dir = direction[0]
    sources = experts // CHUNKS
    part = sources * capacity
    share = rows // experts
    gathered = [
        lax.all_gather(cached_hidden[j * part : (j + 1) * part], "dp", axis=0, tiled=True)
        for j in range(CHUNKS)
    ]
    tables = slot_tables(expert_ids, gate_weights, experts, capacity)
    tables = jnp.broadcast_to(tables[None], (rows,) + tables.shape)
    tables = lax.all_to_all(tables, "dp", split_axis=0, concat_axis=0, tiled=True)
    tables = lax.all_to_all(tables, "expert", split_axis=0, concat_axis=0, tiled=True)
    tables = tables.reshape(CHUNKS, sources, share, 2, experts, capacity)
    tables = tables.transpose(0, 3, 4, 2, 1, 5)
    block = (
        jnp.arange(share, dtype=jnp.float32)[:, None] * sources
        + jnp.arange(sources, dtype=jnp.float32)[None, :]
    )
    keys = tables[:, 0] + (tok_count * block)[None, None, :, :, None]
    keys = keys.reshape(CHUNKS, -1)
    weights = tables[:, 1].reshape(CHUNKS, -1)
    total = None
    for j in range(CHUNKS):
        same = keys[j][:, None] == keys[j][None, :]
        mix = jnp.where(same, (scale * weights[j])[:, None] * weights[j][None, :], 0.0)
        high = lax.reduce_precision(mix, 8, 7)
        low = (mix - high).astype(jnp.bfloat16)
        high = high.astype(jnp.bfloat16)
        block_rows = gathered[j]
        if total is not None:
            block_rows, total = lax.optimization_barrier((block_rows, total))
        tangent = lax.dot_general(
            block_rows, local_dir, (((1,), (1,)), ((), ())), preferred_element_type=jnp.float32
        ).astype(jnp.bfloat16)
        arrived = lax.all_to_all(tangent, "expert", split_axis=0, concat_axis=0, tiled=True)
        adjoint = jnp.dot(high, arrived, preferred_element_type=jnp.float32) + jnp.dot(
            low, arrived, preferred_element_type=jnp.float32
        )
        adjoint = adjoint.astype(jnp.bfloat16)
        back = lax.all_to_all(adjoint, "expert", split_axis=0, concat_axis=0, tiled=True)
        term = lax.dot_general(
            back, block_rows, (((0,), (0,)), ((), ())), preferred_element_type=jnp.float32
        )
        total = term if total is None else total + term
    return total[None]


def solution(mesh):
    return jax.shard_map(
        body,
        mesh=mesh,
        in_specs=(
            P(("dp", "expert"), None),
            P("expert", "dp", None),
            P(("dp", "expert"), None),
            P(("dp", "expert"), None),
        ),
        out_specs=P("expert", "dp", None),
        check_vma=False,
    )
```

time: 338 us -> 351 us (1.038)
  blocking collectives: 63.9 us -> 11.1 us
  starting transfers between devices: 14.3 us -> 62.8 us
  waiting for transfers between devices: 161 us -> 196 us
  local copies, waits for them, and re-layouts: 54 us -> 26.9 us
  matrix products: 15.2 us -> 37.2 us
  other arithmetic: 14.9 us -> 0.43 us
    all_to_all x2 -> x1, blocking collectives: 63.9 us -> 11.1 us  [body(): lax.all_to_all(adjoint, 'expert', split_axis=0, concat_axis=0, tiled=True)]
    all_to_all x2 -> x9, starting transfers between devices: 14.3 us -> 62.7 us  [the longest x4 26.6 us: body(): lax.all_to_all(tangent, 'expert', split_axis=0, concat_axis=0, tiled=True)]
    all_gather x1 -> x4, waiting for transfers between devices: 95 us -> 129 us  [body(): lax.all_gather(cached_hidden[j * part:(j + 1) * part], 'dp', axis=0, tile...]
    dot_general x2 -> x17, matrix products: 15.2 us -> 37.2 us  [the longest x4 11.8 us: body(): lax.dot_general(block_rows, local_dir, (((1,), (1,)), ((), ())), preferre...]
    all_to_all x5 -> x1, local copies, waits for them, and re-layouts: 16 us -> 0.01 us  [body(): lax.all_to_all(tables, 'expert', split_axis=0, concat_axis=0, tiled=True)]
    mul x3 -> x0, local copies, waits for them, and re-layouts: 11.4 us -> none  [body(): outgoing = (gates[..., None] * combined[:, None, :]).astype(jnp.bfloat16)]
    unnamed x9 -> x20, local copies, waits for them, and re-layouts: 14.2 us -> 4.41 us
    convert_element_type x1 -> x8, local copies, waits for them, and re-layouts: 1.41 us -> 10.6 us  [the longest x4 7.16 us: body(): adjoint = adjoint.astype(jnp.bfloat16)]
  transfers between devices with their start and end apart: 3 -> 13, of which waited for: 3 -> 13; matrix products, arithmetic and copies ran while one was open for 1% -> 14% of each run, Pallas kernels for 0% -> 0%
where the time goes in v1:
time: 351 us; the launch traced here: 348 us
  waiting for transfers between devices  196 us (56%)
  starting transfers between devices  62.8 us (18%)
  matrix products  37.2 us (11%)
  local copies, waits for them, and re-layouts  26.9 us (8%)
  between operations  13.4 us (4%)
  blocking collectives  11.1 us (3%)
    all_gather x4, waiting for transfers between devices, body(): lax.all_gather(cached_hidden[j * part:(j + 1) * part], 'dp', axis=0, tile...  129 us
    all_to_all x4, waiting for transfers between devices, body(): lax.all_to_all(tangent, 'expert', split_axis=0, concat_axis=0, tiled=True)  30.5 us
    all_to_all x4, starting transfers between devices, body(): lax.all_to_all(tangent, 'expert', split_axis=0, concat_axis=0, tiled=True)  26.6 us
    all_to_all x1, starting transfers between devices, body(): lax.all_to_all(tables, 'dp', split_axis=0, concat_axis=0, tiled=True)  16.8 us
    all_to_all x3, waiting for transfers between devices, body(): lax.all_to_all(adjoint, 'expert', split_axis=0, concat_axis=0, tiled=True)  16 us
    all_to_all x3, starting transfers between devices, body(): lax.all_to_all(adjoint, 'expert', split_axis=0, concat_axis=0, tiled=True)  12.6 us
    all_to_all x1, waiting for transfers between devices, body(): lax.all_to_all(tables, 'dp', split_axis=0, concat_axis=0, tiled=True)  12 us
    dot_general x4, matrix products, body(): lax.dot_general(block_rows, local_dir, (((1,), (1,)), ((), ())), preferre...  11.8 us
  transfers between devices with their start and end apart: 13, of which 13 were waited for; matrix products, arithmetic and copies ran while one was open for 14% of the time, Pallas kernels for 0%

profile of v1, /device:TPU:1, one launch (start us, length us, event | category | flops | bytes accessed | tf_op | source)
XLA Modules:
  0.0 348.2 jit_solution(11020806377602228993)
XLA Ops:
  6.5 1.8 fusion.53
  13.4 16.8 %all-to-all-start = ((f32[32,2,128]{2,1,0:T(2,128)}), f32[32,2,128]{2,1,0:T(2,128)}, u32[]{:S(2)}, u32[]{:S(2)}) async-start(f32[32,2,128]{2,1,0:T(2,128)} %broadcast_in_dim.58), calls=%async_computation | async-start | bytes 65536 | tf_op jit(solution)/shard_map/all_to_all | solution.py:45
  30.3 12.0 %all-to-all-done = f32[32,2,128]{2,1,0:T(2,128)} async-done(((f32[32,2,128]{2,1,0:T(2,128)}), f32[32,2,128]{2,1,0:T(2,128)}, u32[]{:S(2)}, u32[]{:S(2)}) %all-to-all-start) | async-done | bytes 32800 | tf_op jit(solution)/shard_map/all_to_all | solution.py:45
  42.3 6.8 %all-to-all-start.1 = ((f32[32,2,128]{2,1,0:T(2,128)}), f32[32,2,128]{2,1,0:T(2,128)S(1)}, u32[]{:S(2)}, u32[]{:S(2)}) async-start(f32[32,2,128]{2,1,0:T(2,128)} %all-to-all-done), calls=%async_computation.1 | async-start | bytes 65536 | tf_op jit(solution)/shard_map/all_to_all | solution.py:46
  49.1 6.5 %all-to-all-done.1 = f32[32,2,128]{2,1,0:T(2,128)S(1)} async-done(((f32[32,2,128]{2,1,0:T(2,128)}), f32[32,2,128]{2,1,0:T(2,128)S(1)}, u32[]{:S(2)}, u32[]{:S(2)}) %all-to-all-start.1) | async-done | bytes 32800 | tf_op jit(solution)/shard_map/all_to_all | solution.py:46
  57.6 30.6 %all-gather.11.cloned.1.call-done = bf16[1024,1536]{1,0:T(8,128)(2,1)} async-done(((bf16[32,1536]{1,0:T(8,128)(2,1)}), bf16[1024,1536]{1,0:T(8,128)(2,1)}) %all-gather.11.cloned.1.call-update) | async-done | bytes 3145744 | tf_op jit(solution)/shard_map/all_gather | solution.py:40
  88.2 3.0 convolution_convert_fusion.3
  92.0 6.7 %all-to-all-start.2 = ((bf16[16,64,90]{2,1,0:T(8,128)(2,1)}), bf16[16,64,90]{2,1,0:T(8,128)(2,1)S(1)}, u32[]{:S(2)}, u32[]{:S(2)}) async-start(bf16[16,64,90]{2,1,0:T(8,128)(2,1)} %bitcast.5), calls=%async_computation.2 | async-start | bytes 524288 | tf_op jit(solution)/shard_map/all_to_all | solution.py:69
  98.8 7.6 %all-to-all-done.2 = bf16[16,64,90]{2,1,0:T(8,128)(2,1)S(1)} async-done(((bf16[16,64,90]{2,1,0:T(8,128)(2,1)}), bf16[16,64,90]{2,1,0:T(8,128)(2,1)S(1)}, u32[]{:S(2)}, u32[]{:S(2)}) %all-to-all-start.2) | async-done | bytes 184352 | tf_op jit(solution)/shard_map/all_to_all | solution.py:69
  107.1 1.1 fusion.11
  108.2 2.8 fusion.29
  111.0 1.8 copy.51
  112.8 4.2 %all-to-all-start.3 = ((bf16[16,64,90]{2,1,0:T(8,128)(2,1)}), bf16[16,64,90]{2,1,0:T(8,128)(2,1)}, u32[]{:S(2)}, u32[]{:S(2)}) async-start(bf16[16,64,90]{2,1,0:T(8,128)(2,1)} %bitcast.60), calls=%async_computation.3 | async-start | bytes 524288 | tf_op jit(solution)/shard_map/all_to_all | solution.py:74
  118.0 0.9 copy.52
  119.0 5.3 %all-to-all-done.3 = bf16[16,64,90]{2,1,0:T(8,128)(2,1)} async-done(((bf16[16,64,90]{2,1,0:T(8,128)(2,1)}), bf16[16,64,90]{2,1,0:T(8,128)(2,1)}, u32[]{:S(2)}, u32[]{:S(2)}) %all-to-all-start.3) | async-done | bytes 184352 | tf_op jit(solution)/shard_map/all_to_all | solution.py:74
  124.4 2.4 fusion.55
  126.8 33.0 %all-gather.9.cloned.1.call-done = bf16[1024,1536]{1,0:T(8,128)(2,1)} async-done(((bf16[32,1536]{1,0:T(8,128)(2,1)}), bf16[1024,1536]{1,0:T(8,128)(2,1)}) %all-gather.9.cloned.1.call-update) | async-done | bytes 3145744 | tf_op jit(solution)/shard_map/all_gather | solution.py:40
  159.8 3.0 convolution_convert_fusion.2
  163.6 6.6 %all-to-all-start.4 = ((bf16[16,64,90]{2,1,0:T(8,128)(2,1)}), bf16[16,64,90]{2,1,0:T(8,128)(2,1)S(1)}, u32[]{:S(2)}, u32[]{:S(2)}) async-start(bf16[16,64,90]{2,1,0:T(8,128)(2,1)} %bitcast.9), calls=%async_computation.4 | async-start | bytes 524288 | tf_op jit(solution)/shard_map/all_to_all | solution.py:69
  170.2 7.6 %all-to-all-done.4 = bf16[16,64,90]{2,1,0:T(8,128)(2,1)S(1)} async-done(((bf16[16,64,90]{2,1,0:T(8,128)(2,1)}), bf16[16,64,90]{2,1,0:T(8,128)(2,1)S(1)}, u32[]{:S(2)}, u32[]{:S(2)}) %all-to-all-start.4) | async-done | bytes 184352 | tf_op jit(solution)/shard_map/all_to_all | solution.py:69
  178.5 1.1 fusion.9
  179.6 2.8 fusion.30
  182.4 1.8 copy.55
  184.2 4.2 %all-to-all-start.5 = ((bf16[16,64,90]{2,1,0:T(8,128)(2,1)}), bf16[16,64,90]{2,1,0:T(8,128)(2,1)}, u32[]{:S(2)}, u32[]{:S(2)}) async-start(bf16[16,64,90]{2,1,0:T(8,128)(2,1)} %bitcast.61), calls=%async_computation.5 | async-start | bytes 524288 | tf_op jit(solution)/shard_map/all_to_all | solution.py:74
  188.4 0.9 copy.57
  189.4 0.9 copy.56
  190.4 5.3 %all-to-all-done.5 = bf16[16,64,90]{2,1,0:T(8,128)(2,1)} async-done(((bf16[16,64,90]{2,1,0:T(8,128)(2,1)}), bf16[16,64,90]{2,1,0:T(8,128)(2,1)}, u32[]{:S(2)}, u32[]{:S(2)}) %all-to-all-start.5) | async-done | bytes 184352 | tf_op jit(solution)/shard_map/all_to_all | solution.py:74
  195.8 2.6 convolution_add_fusion.2
  198.4 33.1 %all-gather.7.cloned.1.call-done = bf16[1024,1536]{1,0:T(8,128)(2,1)} async-done(((bf16[32,1536]{1,0:T(8,128)(2,1)}), bf16[1024,1536]{1,0:T(8,128)(2,1)}) %all-gather.7.cloned.1.call-update) | async-done | bytes 3145744 | tf_op jit(solution)/shard_map/all_gather | solution.py:40
  231.5 3.0 convolution_convert_fusion.1
  235.4 6.4 %all-to-all-start.6 = ((bf16[16,64,90]{2,1,0:T(8,128)(2,1)}), bf16[16,64,90]{2,1,0:T(8,128)(2,1)S(1)}, u32[]{:S(2)}, u32[]{:S(2)}) async-start(bf16[16,64,90]{2,1,0:T(8,128)(2,1)} %bitcast.13), calls=%async_computation.6 | async-start | bytes 524288 | tf_op jit(solution)/shard_map/all_to_all | solution.py:69
  241.8 7.6 %all-to-all-done.6 = bf16[16,64,90]{2,1,0:T(8,128)(2,1)S(1)} async-done(((bf16[16,64,90]{2,1,0:T(8,128)(2,1)}), bf16[16,64,90]{2,1,0:T(8,128)(2,1)S(1)}, u32[]{:S(2)}, u32[]{:S(2)}) %all-to-all-start.6) | async-done | bytes 184352 | tf_op jit(solution)/shard_map/all_to_all | solution.py:69
  250.1 1.1 fusion.7
  251.3 2.8 fusion.31
  254.1 1.8 copy.59
  255.9 4.2 %all-to-all-start.7 = ((bf16[16,64,90]{2,1,0:T(8,128)(2,1)}), bf16[16,64,90]{2,1,0:T(8,128)(2,1)}, u32[]{:S(2)}, u32[]{:S(2)}) async-start(bf16[16,64,90]{2,1,0:T(8,128)(2,1)} %bitcast.59), calls=%async_computation.7 | async-start | bytes 524288 | tf_op jit(solution)/shard_map/all_to_all | solution.py:74
  262.1 5.3 %all-to-all-done.7 = bf16[16,64,90]{2,1,0:T(8,128)(2,1)} async-done(((bf16[16,64,90]{2,1,0:T(8,128)(2,1)}), bf16[16,64,90]{2,1,0:T(8,128)(2,1)}, u32[]{:S(2)}, u32[]{:S(2)}) %all-to-all-start.7) | async-done | bytes 184352 | tf_op jit(solution)/shard_map/all_to_all | solution.py:74
  267.4 2.6 convolution_add_fusion.1
  270.1 32.7 %all-gather.5.cloned.1.call-done = bf16[1024,1536]{1,0:T(8,128)(2,1)} async-done(((bf16[32,1536]{1,0:T(8,128)(2,1)}), bf16[1024,1536]{1,0:T(8,128)(2,1)}) %all-gather.5.cloned.1.call-update) | async-done | bytes 3145744 | tf_op jit(solution)/shard_map/all_gather | solution.py:40
  302.8 3.0 convolution_convert_fusion
  306.6 6.8 %all-to-all-start.8 = ((bf16[16,64,90]{2,1,0:T(8,128)(2,1)}), bf16[16,64,90]{2,1,0:T(8,128)(2,1)S(1)}, u32[]{:S(2)}, u32[]{:S(2)}) async-start(bf16[16,64,90]{2,1,0:T(8,128)(2,1)} %bitcast.17), calls=%async_computation.8 | async-start | bytes 524288 | tf_op jit(solution)/shard_map/all_to_all | solution.py:69
  313.5 7.6 %all-to-all-done.8 = bf16[16,64,90]{2,1,0:T(8,128)(2,1)S(1)} async-done(((bf16[16,64,90]{2,1,0:T(8,128)(2,1)}), bf16[16,64,90]{2,1,0:T(8,128)(2,1)S(1)}, u32[]{:S(2)}, u32[]{:S(2)}) %all-to-all-start.8) | async-done | bytes 184352 | tf_op jit(solution)/shard_map/all_to_all | solution.py:69
  321.8 1.1 fusion.5
  323.0 2.8 fusion.32
  325.7 1.8 copy.63
  327.5 11.1 %all_to_all.106 = bf16[16,64,90]{2,1,0:T(8,128)(2,1)S(1)} all-to-all(bf16[16,64,90]{2,1,0:T(8,128)(2,1)} %bitcast.62), channel_id=1, replica_groups=mesh['dp'=32,'expert'=16] {'expert'}, dimensions={0} | all-to-all | bytes 368640 | tf_op jit(solution)/shard_map/all_to_all | solution.py:74
  338.6 1.7 fusion.4
  340.3 1.4 copy.64
  (63 shorter events, 16.6 us)
Async XLA Ops:
  6.5 81.7 %copy-start = (bf16[1,90,1536]{2,1,0:T(8,128)(2,1)S(1)}, bf16[1,90,1536]{2,1,0:T(8,128)(2,1)}, u32[]{:S(2)}) copy-start(bf16[1,90,1536]{2,1,0:T(8,128)(2,1)} %param.5) | copy-start | bytes 829444
  6.5 81.6 %all-gather.11.cloned.1.call-start = ((), (), s32[]{:S(2)}) async-start(), calls=%async_computation.13 | async-start | bytes 3244032 | tf_op jit(solution)/shard_map/all_gather | solution.py:40
  8.4 151.4 %all-gather.9.cloned.1.call-start = ((), (), s32[]{:S(2)}) async-start(), calls=%async_computation.12 | async-start | bytes 3244032 | tf_op jit(solution)/shard_map/all_gather | solution.py:40
  9.1 222.4 %all-gather.7.cloned.1.call-start = ((), (), s32[]{:S(2)}) async-start(), calls=%async_computation.11 | async-start | bytes 3244032 | tf_op jit(solution)/shard_map/all_gather | solution.py:40
  9.9 292.9 %all-gather.5.cloned.1.call-start = ((), (), s32[]{:S(2)}) async-start(), calls=%async_computation.10 | async-start | bytes 3244032 | tf_op jit(solution)/shard_map/all_gather | solution.py:40
  13.4 28.8 %all-to-all-start = ((f32[32,2,128]{2,1,0:T(2,128)}), f32[32,2,128]{2,1,0:T(2,128)}, u32[]{:S(2)}, u32[]{:S(2)}) async-start(f32[32,2,128]{2,1,0:T(2,128)} %broadcast_in_dim.58), calls=%async_computation | async-start | bytes 65536 | tf_op jit(solution)/shard_map/all_to_all | solution.py:45
  42.3 13.2 %all-to-all-start.1 = ((f32[32,2,128]{2,1,0:T(2,128)}), f32[32,2,128]{2,1,0:T(2,128)S(1)}, u32[]{:S(2)}, u32[]{:S(2)}) async-start(f32[32,2,128]{2,1,0:T(2,128)} %all-to-all-done), calls=%async_computation.1 | async-start | bytes 65536 | tf_op jit(solution)/shard_map/all_to_all | solution.py:46
  92.0 14.4 %all-to-all-start.2 = ((bf16[16,64,90]{2,1,0:T(8,128)(2,1)}), bf16[16,64,90]{2,1,0:T(8,128)(2,1)S(1)}, u32[]{:S(2)}, u32[]{:S(2)}) async-start(bf16[16,64,90]{2,1,0:T(8,128)(2,1)} %bitcast.5), calls=%async_computation.2 | async-start | bytes 524288 | tf_op jit(solution)/shard_map/all_to_all | solution.py:69
  106.4 0.7 copy-start.5
  108.2 16.1 %copy-start.4 = (bf16[1024,1536]{1,0:T(8,128)(2,1)S(1)}, bf16[1024,1536]{1,0:T(8,128)(2,1)}, u32[]{:S(2)}) copy-start(bf16[1024,1536]{1,0:T(8,128)(2,1)} %all-gather.11.cloned.1.call-done) | copy-start | bytes 9437188
  112.8 11.5 %all-to-all-start.3 = ((bf16[16,64,90]{2,1,0:T(8,128)(2,1)}), bf16[16,64,90]{2,1,0:T(8,128)(2,1)}, u32[]{:S(2)}, u32[]{:S(2)}) async-start(bf16[16,64,90]{2,1,0:T(8,128)(2,1)} %bitcast.60), calls=%async_computation.3 | async-start | bytes 524288 | tf_op jit(solution)/shard_map/all_to_all | solution.py:74
  163.6 14.2 %all-to-all-start.4 = ((bf16[16,64,90]{2,1,0:T(8,128)(2,1)}), bf16[16,64,90]{2,1,0:T(8,128)(2,1)S(1)}, u32[]{:S(2)}, u32[]{:S(2)}) async-start(bf16[16,64,90]{2,1,0:T(8,128)(2,1)} %bitcast.9), calls=%async_computation.4 | async-start | bytes 524288 | tf_op jit(solution)/shard_map/all_to_all | solution.py:69
  177.8 0.7 copy-start.6
  179.6 16.1 %copy-start.3 = (bf16[1024,1536]{1,0:T(8,128)(2,1)S(1)}, bf16[1024,1536]{1,0:T(8,128)(2,1)}, u32[]{:S(2)}) copy-start(bf16[1024,1536]{1,0:T(8,128)(2,1)} %all-gather.9.cloned.1.call-done) | copy-start | bytes 9437188
  184.2 11.5 %all-to-all-start.5 = ((bf16[16,64,90]{2,1,0:T(8,128)(2,1)}), bf16[16,64,90]{2,1,0:T(8,128)(2,1)}, u32[]{:S(2)}, u32[]{:S(2)}) async-start(bf16[16,64,90]{2,1,0:T(8,128)(2,1)} %bitcast.61), calls=%async_computation.5 | async-start | bytes 524288 | tf_op jit(solution)/shard_map/all_to_all | solution.py:74
  235.4 14.1 %all-to-all-start.6 = ((bf16[16,64,90]{2,1,0:T(8,128)(2,1)}), bf16[16,64,90]{2,1,0:T(8,128)(2,1)S(1)}, u32[]{:S(2)}, u32[]{:S(2)}) async-start(bf16[16,64,90]{2,1,0:T(8,128)(2,1)} %bitcast.13), calls=%async_computation.6 | async-start | bytes 524288 | tf_op jit(solution)/shard_map/all_to_all | solution.py:69
  249.4 0.7 copy-start.7
  251.3 16.2 %copy-start.2 = (bf16[1024,1536]{1,0:T(8,128)(2,1)S(1)}, bf16[1024,1536]{1,0:T(8,128)(2,1)}, u32[]{:S(2)}) copy-start(bf16[1024,1536]{1,0:T(8,128)(2,1)} %all-gather.7.cloned.1.call-done) | copy-start | bytes 9437188
  255.9 11.5 %all-to-all-start.7 = ((bf16[16,64,90]{2,1,0:T(8,128)(2,1)}), bf16[16,64,90]{2,1,0:T(8,128)(2,1)}, u32[]{:S(2)}, u32[]{:S(2)}) async-start(bf16[16,64,90]{2,1,0:T(8,128)(2,1)} %bitcast.59), calls=%async_computation.7 | async-start | bytes 524288 | tf_op jit(solution)/shard_map/all_to_all | solution.py:74
  306.6 14.5 %all-to-all-start.8 = ((bf16[16,64,90]{2,1,0:T(8,128)(2,1)}), bf16[16,64,90]{2,1,0:T(8,128)(2,1)S(1)}, u32[]{:S(2)}, u32[]{:S(2)}) async-start(bf16[16,64,90]{2,1,0:T(8,128)(2,1)} %bitcast.17), calls=%async_computation.8 | async-start | bytes 524288 | tf_op jit(solution)/shard_map/all_to_all | solution.py:69
  321.1 0.7 copy-start.8
  322.9 15.6 %copy-start.1 = (bf16[1024,1536]{1,0:T(8,128)(2,1)S(1)}, bf16[1024,1536]{1,0:T(8,128)(2,1)}, u32[]{:S(2)}) copy-start(bf16[1024,1536]{1,0:T(8,128)(2,1)} %all-gather.5.cloned.1.call-done) | copy-start | bytes 9437188
Sparse Core Ops, SparseCore 0:
  9.5 78.6 all-gather.10
  90.3 69.4 all-gather.8
  161.9 69.5 all-gather.6
  233.5 69.2 all-gather.4
